TPU v7x, 128 devices: a whole 4x4x4 slice. The times are simulated.
128 devices in a mesh: row: 8 (over z, core), col: 16 (over y, x).
Axes of the slice: x: 4, y: 4, z: 4, core: 2. Of those that a mesh axis runs over, the one named last changes fastest.
Arguments:
- kernel: float32 [16384, 16384], P('row', 'col'), may hold values from 0 to 3, as said below
Outputs:
- trailing: float32 [16384, 16384], P('row', 'col')
- factor_t: float32 [1024, 16384], P('col', 'row')
Inputs may be any that keep to these rules, and one draw needn't show every extreme that they name: K is symmetric: an RBF kernel over 256 donor features plus each donor's noise variance, of 0.5 or more, on the diagonal.
All inputs are finite; a program needn't handle non-finite values.
Results may differ from a plain program's by a relative error of at most 0.0003.
Values sent between devices are 32-bit elements; how exact they have to be, the bound alone decides.
A program may use at most 128 MiB of HBM per device.

v0:
```python
import jax
import jax.numpy as jnp
from jax import lax
from jax.sharding import PartitionSpec as P

PANEL = 512
PANELS = 2
TILE = 32
HIGHEST = lax.Precision.HIGHEST


def mm(a, b):
    return jnp.dot(a, b, precision=HIGHEST, preferred_element_type=jnp.float32)


def mm_tn(a, b):
    return lax.dot_general(
        a, b, (((0,), (0,)), ((), ())), precision=HIGHEST, preferred_element_type=jnp.float32
    )


def mm_nt(a, b):
    return lax.dot_general(
        a, b, (((1,), (1,)), ((), ())), precision=HIGHEST, preferred_element_type=jnp.float32
    )


def tri_inverse(lower):
    eye = jnp.eye(lower.shape[0], dtype=lower.dtype)
    return jax.scipy.linalg.solve_triangular(lower, eye, lower=True)


def sym_chol(block):
    return jnp.linalg.cholesky(block)


def local(kernel):
    grid_rows = lax.axis_size("row")
    grid_cols = lax.axis_size("col")
    my_row = lax.axis_index("row")
    my_col = lax.axis_index("col")
    rows_loc, cols_loc = kernel.shape
    lead = PANELS * PANEL
    lead_rt = lead // (TILE * grid_rows)
    lead_ct = lead // (TILE * grid_cols)
    lead_r = lead_rt * TILE
    lead_c = lead_ct * TILE
    row_local = jnp.arange(rows_loc, dtype=jnp.int32)
    row_ids = (row_local // TILE * grid_rows + my_row) * TILE + row_local % TILE
    col_local = jnp.arange(cols_loc, dtype=jnp.int32)
    col_ids = (col_local // TILE * grid_cols + my_col) * TILE + col_local % TILE
    corner = kernel[:lead_r, :lead_c].reshape(1, lead_r * lead_c)
    blocks = lax.all_gather(corner, ("row", "col"), axis=0, tiled=True)
    blocks = blocks.reshape(grid_rows, grid_cols, lead_rt, TILE, lead_ct, TILE)
    a_lead = blocks.transpose(2, 0, 3, 4, 1, 5).reshape(lead, lead)
    cols_part = lax.all_gather(kernel[:, :lead_c], "col", axis=1, tiled=True)
    cols_part = cols_part.reshape(rows_loc, grid_cols, lead_ct, TILE)
    x_rows = cols_part.transpose(0, 2, 1, 3).reshape(rows_loc, lead)
    rows_part = lax.all_gather(kernel[:lead_r, :], "row", axis=0, tiled=True)
    rows_part = rows_part.reshape(grid_rows, lead_rt, TILE, cols_loc)
    y_cols = rows_part.transpose(1, 0, 2, 3).reshape(lead, cols_loc)
    a00 = a_lead[:PANEL, :PANEL]
    a01 = a_lead[:PANEL, PANEL:]
    a11 = a_lead[PANEL:, PANEL:]
    l0 = sym_chol(a00)
    l0inv = tri_inverse(l0)
    g0p1 = mm(l0inv, a01)
    s11 = a11 - mm_tn(g0p1, g0p1)
    l1 = sym_chol(s11)
    l1inv = tri_inverse(l1)

    def factor(panel_t, ids):
        g0 = mm(l0inv, panel_t[:PANEL])
        s1 = panel_t[PANEL:] - mm_tn(g0p1, g0)
        g1 = mm(l1inv, s1)
        g1 = jnp.where(ids[None, :] >= PANEL, g1, 0.0)
        return jnp.concatenate([g0, g1], axis=0)

    g_rows = factor(x_rows.T, row_ids)
    g_cols = factor(y_cols, col_ids)
    schur = kernel - mm_tn(g_rows, g_cols)
    keep = (row_ids[:, None] >= lead) & (col_ids[None, :] >= lead)
    trailing = jnp.where(keep, schur, 0.0)
    per_col = lead // grid_cols
    factor_out = lax.dynamic_slice_in_dim(g_rows, my_col * per_col, per_col, 0)
    return (trailing, factor_out)


def solution(mesh):
    return jax.shard_map(
        local,
        mesh=mesh,
        in_specs=(P("row", "col"),),
        out_specs=(P("row", "col"), P("col", "row")),
        check_vma=False,
    )
```

profile of v0, /device:TPU:1, one launch (start us, length us, event | category | flops | bytes accessed | tf_op | source)
XLA Modules:
  0.0 584.9 jit_solution(12073595241916444088)
XLA Ops:
  12.2 34.1 %all-gather.7.cloned.1.call-done = f32[1024,1024]{1,0:T(8,128)} async-done(((f32[128,1024]{1,0:T(8,128)}), f32[1024,1024]{1,0:T(8,128)}) %all-gather.7.cloned.1.call-update) | async-done | bytes 4194320 | tf_op jit(solution)/shard_map/all_gather | solution.py:59
  51.7 65.0 %all-gather.9.cloned.1.call-done = f32[128,1,8192]{2,1,0:T(1,128)} async-done(((f32[1,1,8192]{2,1,0:T(1,128)}), f32[128,1,8192]{2,1,0:T(1,128)}) %all-gather.9.cloned.1.call-update) | async-done | bytes 4194320 | tf_op jit(solution)/shard_map/all_gather | solution.py:53
  116.7 13.2 %reduce.16 = f32[128,8192]{1,0:T(8,128)} reduce(f32[128,1,8192]{2,1,0:T(1,128)} %all-gather.9.cloned.1.call-done, f32[]{:T(128)} %constant.211), dimensions={1}, to_apply=%all-gather.reduce_sub_computation | reduce | bytes 8388612 | tf_op jit(solution)/shard_map/all_gather | solution.py:53
  129.9 16.6 %reshape.139 = f32[8,16,4,32,2,32]{5,4,3,2,1,0:T(2,128)} reshape(f32[128,8192]{1,0:T(8,128)} %reduce.16) | data formatting | bytes 8388608 | tf_op jit(solution)/shard_map/reshape | solution.py:54
  146.5 26.1 %copy.20 = f32[4,8,32,2,16,32]{2,1,0,5,4,3:T(8,128)} copy(f32[4,8,32,2,16,32]{5,3,2,0,4,1:T(2,128)} %bitcast.121) | data formatting | bytes 8388608 | tf_op jit(solution)/shard_map/transpose | solution.py:55
  172.6 14.3 %reshape.140 = f32[1024,1024]{0,1:T(8,128)} reshape(f32[4,8,32,2,16,32]{2,1,0,5,4,3:T(8,128)} %copy.20) | data formatting | bytes 8388608 | tf_op jit(solution)/shard_map/reshape | solution.py:55
  193.2 11.7 %cholesky.286 = f32[128,128]{1,0:T(8,128)S(1)} custom-call(f32[128,128]{1,0:T(8,128)S(1)} %cholesky.426), custom_call_target="Cholesky" | custom-call | tf_op jit(solution)/shard_map/jit(cholesky)/cholesky | solution.py:34
  204.9 9.8 %custom-call.27 = f32[1,128,128]{1,2,0:T(8,128)S(1)} custom-call(f32[1,128,128]{2,1,0:T(8,128)S(1)} %get-tuple-element.61), custom_call_target="InvertDiagBlocksLowerTriangular" | custom-call | tf_op jit(solution)/shard_map/jit(cholesky)/cholesky | solution.py:34
  217.4 11.7 %cholesky.305 = f32[128,128]{1,0:T(8,128)S(1)} custom-call(f32[128,128]{1,0:T(8,128)S(1)} %cholesky.430), custom_call_target="Cholesky" | custom-call | tf_op jit(solution)/shard_map/jit(cholesky)/cholesky | solution.py:34
  229.1 10.0 %custom-call.28 = f32[1,128,128]{1,2,0:T(8,128)S(1)} custom-call(f32[1,128,128]{2,1,0:T(8,128)S(1)} %get-tuple-element.58), custom_call_target="InvertDiagBlocksLowerTriangular" | custom-call | tf_op jit(solution)/shard_map/jit(cholesky)/cholesky | solution.py:34
  240.7 11.7 %cholesky.326 = f32[128,128]{1,0:T(8,128)S(1)} custom-call(f32[128,128]{1,0:T(8,128)S(1)} %cholesky.435), custom_call_target="Cholesky" | custom-call | tf_op jit(solution)/shard_map/jit(cholesky)/cholesky | solution.py:34
  252.4 9.8 %custom-call.29 = f32[1,128,128]{1,2,0:T(8,128)S(1)} custom-call(f32[1,128,128]{2,1,0:T(8,128)S(1)} %get-tuple-element.55), custom_call_target="InvertDiagBlocksLowerTriangular" | custom-call | tf_op jit(solution)/shard_map/jit(cholesky)/cholesky | solution.py:34
  263.7 11.7 %cholesky.343 = f32[128,128]{1,0:T(8,128)S(1)} custom-call(f32[128,128]{1,0:T(8,128)S(1)} %convolution_subtract_fusion.12), custom_call_target="Cholesky" | custom-call | tf_op jit(solution)/shard_map/jit(cholesky)/cholesky | solution.py:34
  281.6 12.0 %while.4 = (s32[]{:T(128)}, f32[512,512]{1,0:T(8,128)}, s32[4,2]{0,1:T(2,128)S(1)}, f32[4,128,128]{2,1,0:T(8,128)S(1)}, s32[]{:T(128)}) while((s32[]{:T(128)}, f32[512,512]{1,0:T(8,128)}, s32[4,2]{0,1:T(2,128)S(1)}, f32[4,128,128]{2,1,0:T(8,128)S(1)}, s32[]{:T(128)}) %tuple.58), condition=%wide.while_cond, body=%wide.while_body.sunk | while | flops 2 | bytes 131181 | solution.py:30
  293.7 39.3 %custom-call.30 = f32[4,128,128]{1,2,0:T(8,128)S(1)} custom-call(f32[4,128,128]{2,1,0:T(8,128)S(1)} %get-tuple-element.18), custom_call_target="InvertDiagBlocksLowerTriangular" | custom-call | tf_op jit(solution)/shard_map/jit(_solve_triangular)/triangular_solve | solution.py:30
  349.1 11.7 %cholesky.358 = f32[128,128]{1,0:T(8,128)S(1)} custom-call(f32[128,128]{1,0:T(8,128)S(1)} %cholesky.439), custom_call_target="Cholesky" | custom-call | tf_op jit(solution)/shard_map/jit(cholesky)/cholesky | solution.py:34
  362.0 10.0 %custom-call.31 = f32[1,128,128]{1,2,0:T(8,128)S(1)} custom-call(f32[1,128,128]{2,1,0:T(8,128)S(1)} %get-tuple-element.51), custom_call_target="InvertDiagBlocksLowerTriangular" | custom-call | tf_op jit(solution)/shard_map/jit(cholesky)/cholesky | solution.py:34
  375.1 11.7 %cholesky.377 = f32[128,128]{1,0:T(8,128)S(1)} custom-call(f32[128,128]{1,0:T(8,128)S(1)} %cholesky.443), custom_call_target="Cholesky" | custom-call | tf_op jit(solution)/shard_map/jit(cholesky)/cholesky | solution.py:34
  399.7 11.7 %cholesky.398 = f32[128,128]{1,0:T(8,128)S(1)} custom-call(f32[128,128]{1,0:T(8,128)S(1)} %cholesky.448), custom_call_target="Cholesky" | custom-call | tf_op jit(solution)/shard_map/jit(cholesky)/cholesky | solution.py:34
  412.0 10.0 %custom-call.33 = f32[1,128,128]{1,2,0:T(8,128)S(1)} custom-call(f32[1,128,128]{2,1,0:T(8,128)S(1)} %get-tuple-element.45), custom_call_target="InvertDiagBlocksLowerTriangular" | custom-call | tf_op jit(solution)/shard_map/jit(cholesky)/cholesky | solution.py:34
  424.3 11.7 %cholesky.415 = f32[128,128]{1,0:T(8,128)S(1)} custom-call(f32[128,128]{1,0:T(8,128)S(1)} %convolution_subtract_fusion.11), custom_call_target="Cholesky" | custom-call | tf_op jit(solution)/shard_map/jit(cholesky)/cholesky | solution.py:34
  444.4 11.7 %while.5 = (s32[]{:T(128)}, f32[512,512]{1,0:T(8,128)}, s32[4,2]{0,1:T(2,128)S(1)}, f32[4,128,128]{2,1,0:T(8,128)S(1)}, s32[]{:T(128)}) while((s32[]{:T(128)}, f32[512,512]{1,0:T(8,128)}, s32[4,2]{0,1:T(2,128)S(1)}, f32[4,128,128]{2,1,0:T(8,128)S(1)}, s32[]{:T(128)}) %tuple.70), condition=%wide.while_cond.clone, body=%wide.while_body.clone.sunk | while | flops 2 | bytes 131181 | solution.py:30
  456.1 39.7 %custom-call.34 = f32[4,128,128]{1,2,0:T(8,128)S(1)} custom-call(f32[4,128,128]{2,1,0:T(8,128)S(1)} %get-tuple-element.19), custom_call_target="InvertDiagBlocksLowerTriangular" | custom-call | tf_op jit(solution)/shard_map/jit(_solve_triangular)/triangular_solve | solution.py:30
  546.5 31.7 %subtract_select_fusion = f32[2048,1024]{1,0:T(8,128)} fusion(f32[2048,1024]{1,0:T(8,128)} %param.4, pred[1024]{0:T(1024)(128)(4,1)S(1)} %get-tuple-element.67, pred[2048]{0:T(1024)(128)(4,1)S(1)} %get-tuple-element.69, f32[512,1024]{1,0:T(8,128)S(1)} %copy-done.11, f32[512,1024]{1,0:T(8,128)S(1)} %copy-done.3, f32[512,2048]{1,0:T(8,128)S(1)} %fusion.7, ...), kind=kOutput, calls=%fused_computation.8 | convolution fusion | flops 25779240960 | bytes 29363200 | tf_op jit(solution)/shard_map/dot_general | solution.py:17
  (140 shorter events, 141.8 us)
Async XLA Ops:
  7.2 3.7 slice-start
  7.2 39.1 %all-gather.7.cloned.1.call-start = ((), (), s32[]{:S(2)}) async-start(), calls=%async_computation.1 | async-start | bytes 4718592 | tf_op jit(solution)/shard_map/all_gather | solution.py:59
  9.2 107.5 %all-gather.9.cloned.1.call-start = ((), (), s32[]{:S(2)}) async-start(), calls=%async_computation.2 | async-start | bytes 4227072 | tf_op jit(solution)/shard_map/all_gather | solution.py:53
  10.8 507.1 %all-gather.5.cloned.1.call-start = ((), (), s32[]{:S(2)}) async-start(), calls=%async_computation | async-start | bytes 8912896 | tf_op jit(solution)/shard_map/all_gather | solution.py:56
  192.2 1.0 copy-start.10
  333.0 6.0 %copy-start = (f32[1024,1024]{0,1:T(8,128)S(1)}, f32[1024,1024]{0,1:T(8,128)}, u32[]{:S(2)}) copy-start(f32[1024,1024]{0,1:T(8,128)} %reshape.140) | copy-start | bytes 12582916
  339.1 7.3 %copy-start.7 = (f32[128,512]{1,0:T(8,128)}, f32[128,512]{1,0:T(8,128)S(1)}, u32[]{:S(2)}) copy-start(f32[128,512]{1,0:T(8,128)S(1)} %fusion.59) | copy-start | bytes 786436
  348.1 1.0 copy-start.9
  495.8 0.7 copy-start.12
  495.8 8.9 %copy-start.4 = (f32[2,8,32,1024]{3,2,1,0:T(8,128)S(1)}, f32[2,8,32,1024]{3,2,1,0:T(8,128)}, u32[]{:S(2)}) copy-start(f32[2,8,32,1024]{3,2,1,0:T(8,128)} %copy.26) | copy-start | bytes 6291460
  500.4 8.9 %copy-start.1 = (f32[2,8,32,1024]{3,2,1,0:T(8,128)S(1)}, f32[2,8,32,1024]{3,2,1,0:T(8,128)}, u32[]{:S(2)}) copy-start(f32[2,8,32,1024]{3,2,1,0:T(8,128)} %copy.27) | copy-start | bytes 6291460
  501.8 11.1 %copy-start.5 = (f32[128,512]{1,0:T(8,128)}, f32[128,512]{1,0:T(8,128)S(1)}, u32[]{:S(2)}) copy-start(f32[128,512]{1,0:T(8,128)S(1)} %fusion.54) | copy-start | bytes 786436
  509.3 3.5 copy-start.2
  517.9 4.0 copy-start.8
  529.1 7.8 %copy-start.6 = (f32[128,512]{1,0:T(8,128)S(1)}, f32[128,512]{1,0:T(8,128)}, u32[]{:S(2)}) copy-start(f32[128,512]{1,0:T(8,128)} %copy-done.5) | copy-start | bytes 786436
  544.0 1.8 copy-start.3
  544.1 2.4 copy-start.11
Sparse Core Ops, SparseCore 0:
  10.3 35.9 all-gather.6
  50.0 66.6 all-gather.8
  118.9 67.6 all-gather.4
where the time goes:
time: 592 us; the launch traced here: 585 us
  other arithmetic  260 us (44%)
  local copies, waits for them, and re-layouts  106 us (18%)
  matrix products  99.3 us (17%)
  waiting for transfers between devices  99.1 us (17%)
  between operations  19.9 us (3%)
    another operation x29, other arithmetic, sym_chol(): return jnp.linalg.cholesky(block)  160 us
    another operation x5, other arithmetic, tri_inverse(): return jax.scipy.linalg.solve_triangular(lower, eye, lower=True)  82.9 us
    all_gather x1, waiting for transfers between devices, local(): blocks = lax.all_gather(corner, ('row', 'col'), axis=0, tiled=True)  65 us
    dot_general x4, matrix products, mm_tn(): lax.dot_general(a, b, (((0,), (0,)), ((), ())), precision=HIGHEST, prefer...  45.8 us
    all_gather x1, waiting for transfers between devices, local(): rows_part = lax.all_gather(kernel[:lead_r, :], 'row', axis=0, tiled=True)  34.1 us
    transpose x1, local copies, waits for them, and re-layouts, local(): a_lead = blocks.transpose(2, 0, 3, 4, 1, 5).reshape(lead, lead)  26.1 us
    dot_general x5, matrix products, mm(): return jnp.dot(a, b, precision=HIGHEST, preferred_element_type=jnp.float32)  25.8 us
    another operation x27, local copies, waits for them, and re-layouts, tri_inverse(): return jax.scipy.linalg.solve_triangular(lower, eye, lower=True)  23.6 us
  transfers between devices with their start and end apart: 3, of which 2 were waited for; matrix products, arithmetic and copies ran while one was open for 69% of the time, Pallas kernels for 0%

commit v1 on v0

--- a/solution.py
+++ b/solution.py
@@ -56,7 +56,32 @@
     cols_part = lax.all_gather(kernel[:, :lead_c], "col", axis=1, tiled=True)
     cols_part = cols_part.reshape(rows_loc, grid_cols, lead_ct, TILE)
     x_rows = cols_part.transpose(0, 2, 1, 3).reshape(rows_loc, lead)
-    rows_part = lax.all_gather(kernel[:lead_r, :], "row", axis=0, tiled=True)
+
+    def pass_the_yards(raw, array_axis=0):
+        big, clean, state_next = (lax.psum(1, "row"), lax.axis_index("row"), raw.shape[array_axis])
+        steps_seen = [(d, (d + 1) % big) for d in range(big)]
+        cards = [(d, (d - 1) % big) for d in range(big)]
+        w2 = jnp.zeros(
+            (*raw.shape[:array_axis], big * state_next, *raw.shape[array_axis + 1 :]), raw.dtype
+        )
+        w2 = lax.dynamic_update_slice_in_dim(w2, raw, clean * state_next, axis=array_axis)
+        odd = v_next = raw
+        y_new = big // 2
+        tick = 1
+        while tick < y_new + 1:
+            odd = lax.ppermute(odd, "row", steps_seen)
+            w2 = lax.dynamic_update_slice_in_dim(
+                w2, odd, (clean - tick) % big * state_next, axis=array_axis
+            )
+            if tick < big - y_new:
+                v_next = lax.ppermute(v_next, "row", cards)
+                w2 = lax.dynamic_update_slice_in_dim(
+                    w2, v_next, (clean + tick) % big * state_next, axis=array_axis
+                )
+            tick = tick + 1
+        return w2
+
+    rows_part = pass_the_yards(kernel[:lead_r, :])
     rows_part = rows_part.reshape(grid_rows, lead_rt, TILE, cols_loc)
     y_cols = rows_part.transpose(1, 0, 2, 3).reshape(lead, cols_loc)
     a00 = a_lead[:PANEL, :PANEL]

time: 592 us -> 558 us (0.943)
  waiting for transfers between devices: 99.1 us -> 41.5 us
  starting transfers between devices: 0.12 us -> 12.3 us
  local copies, waits for them, and re-layouts: 106 us -> 117 us
    all_gather x1, waiting for transfers between devices: 65 us -> 25.8 us  [local(): blocks = lax.all_gather(corner, ('row', 'col'), axis=0, tiled=True)]
    all_gather x1 -> x0, waiting for transfers between devices: 34.1 us -> none  [local(): rows_part = lax.all_gather(kernel[:lead_r, :], 'row', axis=0, tiled=True)]
    ppermute x0 -> x7, waiting for transfers between devices: none -> 15.7 us  [the longest x4 15.6 us: pass_the_yards(): odd = lax.ppermute(odd, 'row', steps_seen)]
    ppermute x0 -> x7, starting transfers between devices: none -> 12.2 us  [the longest x4 10.5 us: pass_the_yards(): odd = lax.ppermute(odd, 'row', steps_seen)]
    dynamic_update_slice x0 -> x7, local copies, waits for them, and re-layouts: none -> 7.91 us  [the longest x4 5.43 us: pass_the_yards(): lax.dynamic_update_slice_in_dim(w2, odd, (clean - tick) % big * state_nex...]
  transfers between devices with their start and end apart: 3 -> 9, of which waited for: 2 -> 6; matrix products, arithmetic and copies ran while one was open for 69% -> 75% of each run, Pallas kernels for 0% -> 0%
where the time goes in v1:
time: 558 us; the launch traced here: 550 us
  other arithmetic  260 us (47%)
  local copies, waits for them, and re-layouts  117 us (21%)
  matrix products  99.4 us (18%)
  waiting for transfers between devices  41.5 us (7%)
  between operations  20.2 us (4%)
  starting transfers between devices  12.3 us (2%)
    another operation x29, other arithmetic, sym_chol(): return jnp.linalg.cholesky(block)  160 us
    another operation x5, other arithmetic, tri_inverse(): return jax.scipy.linalg.solve_triangular(lower, eye, lower=True)  82.9 us
    dot_general x4, matrix products, mm_tn(): lax.dot_general(a, b, (((0,), (0,)), ((), ())), precision=HIGHEST, prefer...  45.8 us
    transpose x1, local copies, waits for them, and re-layouts, local(): a_lead = blocks.transpose(2, 0, 3, 4, 1, 5).reshape(lead, lead)  26.1 us
    all_gather x1, waiting for transfers between devices, local(): blocks = lax.all_gather(corner, ('row', 'col'), axis=0, tiled=True)  25.8 us
    dot_general x5, matrix products, mm(): return jnp.dot(a, b, precision=HIGHEST, preferred_element_type=jnp.float32)  25.8 us
    another operation x27, local copies, waits for them, and re-layouts, tri_inverse(): return jax.scipy.linalg.solve_triangular(lower, eye, lower=True)  23.6 us
    reshape x1, local copies, waits for them, and re-layouts, local(): blocks = blocks.reshape(grid_rows, grid_cols, lead_rt, TILE, lead_ct, TILE)  16.6 us
  transfers between devices with their start and end apart: 9, of which 6 were waited for; matrix products, arithmetic and copies ran while one was open for 75% of the time, Pallas kernels for 0%

profile of v1, /device:TPU:1, one launch (start us, length us, event | category | flops | bytes accessed | tf_op | source)
XLA Modules:
  0.0 550.3 jit_solution(8823926093509423216)
XLA Ops:
  56.0 25.8 %all-gather.6.cloned.1.call-done = f32[128,1,8192]{2,1,0:T(1,128)} async-done(((f32[1,1,8192]{2,1,0:T(1,128)}), f32[128,1,8192]{2,1,0:T(1,128)}) %all-gather.6.cloned.1.call-update) | async-done | bytes 4194320 | tf_op jit(solution)/shard_map/all_gather | solution.py:53
  81.8 13.2 %reduce.16 = f32[128,8192]{1,0:T(8,128)} reduce(f32[128,1,8192]{2,1,0:T(1,128)} %all-gather.6.cloned.1.call-done, f32[]{:T(128)} %constant.262), dimensions={1}, to_apply=%all-gather.reduce_sub_computation | reduce | bytes 8388612 | tf_op jit(solution)/shard_map/all_gather | solution.py:53
  95.0 16.6 %reshape.139 = f32[8,16,4,32,2,32]{5,4,3,2,1,0:T(2,128)} reshape(f32[128,8192]{1,0:T(8,128)} %reduce.16) | data formatting | bytes 8388608 | tf_op jit(solution)/shard_map/reshape | solution.py:54
  111.6 26.1 %copy.20 = f32[4,8,32,2,16,32]{2,1,0,5,4,3:T(8,128)} copy(f32[4,8,32,2,16,32]{5,3,2,0,4,1:T(2,128)} %bitcast.121) | data formatting | bytes 8388608 | tf_op jit(solution)/shard_map/transpose | solution.py:55
  137.6 14.3 %reshape.140 = f32[1024,1024]{0,1:T(8,128)} reshape(f32[4,8,32,2,16,32]{2,1,0,5,4,3:T(8,128)} %copy.20) | data formatting | bytes 8388608 | tf_op jit(solution)/shard_map/reshape | solution.py:55
  158.2 11.7 %cholesky.286 = f32[128,128]{1,0:T(8,128)S(1)} custom-call(f32[128,128]{1,0:T(8,128)S(1)} %cholesky.426), custom_call_target="Cholesky" | custom-call | tf_op jit(solution)/shard_map/jit(cholesky)/cholesky | solution.py:34
  170.0 9.8 %custom-call.27 = f32[1,128,128]{1,2,0:T(8,128)S(1)} custom-call(f32[1,128,128]{2,1,0:T(8,128)S(1)} %get-tuple-element.63), custom_call_target="InvertDiagBlocksLowerTriangular" | custom-call | tf_op jit(solution)/shard_map/jit(cholesky)/cholesky | solution.py:34
  182.4 11.7 %cholesky.305 = f32[128,128]{1,0:T(8,128)S(1)} custom-call(f32[128,128]{1,0:T(8,128)S(1)} %cholesky.430), custom_call_target="Cholesky" | custom-call | tf_op jit(solution)/shard_map/jit(cholesky)/cholesky | solution.py:34
  194.2 10.0 %custom-call.28 = f32[1,128,128]{1,2,0:T(8,128)S(1)} custom-call(f32[1,128,128]{2,1,0:T(8,128)S(1)} %get-tuple-element.60), custom_call_target="InvertDiagBlocksLowerTriangular" | custom-call | tf_op jit(solution)/shard_map/jit(cholesky)/cholesky | solution.py:34
  205.7 11.7 %cholesky.326 = f32[128,128]{1,0:T(8,128)S(1)} custom-call(f32[128,128]{1,0:T(8,128)S(1)} %cholesky.435), custom_call_target="Cholesky" | custom-call | tf_op jit(solution)/shard_map/jit(cholesky)/cholesky | solution.py:34
  217.5 9.8 %custom-call.29 = f32[1,128,128]{1,2,0:T(8,128)S(1)} custom-call(f32[1,128,128]{2,1,0:T(8,128)S(1)} %get-tuple-element.57), custom_call_target="InvertDiagBlocksLowerTriangular" | custom-call | tf_op jit(solution)/shard_map/jit(cholesky)/cholesky | solution.py:34
  228.7 11.7 %cholesky.343 = f32[128,128]{1,0:T(8,128)S(1)} custom-call(f32[128,128]{1,0:T(8,128)S(1)} %convolution_subtract_fusion.12), custom_call_target="Cholesky" | custom-call | tf_op jit(solution)/shard_map/jit(cholesky)/cholesky | solution.py:34
  246.7 12.0 %while.4 = (s32[]{:T(128)}, f32[512,512]{1,0:T(8,128)}, s32[4,2]{0,1:T(2,128)S(1)}, f32[4,128,128]{2,1,0:T(8,128)S(1)}, s32[]{:T(128)}) while((s32[]{:T(128)}, f32[512,512]{1,0:T(8,128)}, s32[4,2]{0,1:T(2,128)S(1)}, f32[4,128,128]{2,1,0:T(8,128)S(1)}, s32[]{:T(128)}) %tuple.59), condition=%wide.while_cond, body=%wide.while_body.sunk | while | flops 2 | bytes 131181 | solution.py:30
  258.7 39.3 %custom-call.30 = f32[4,128,128]{1,2,0:T(8,128)S(1)} custom-call(f32[4,128,128]{2,1,0:T(8,128)S(1)} %get-tuple-element.18), custom_call_target="InvertDiagBlocksLowerTriangular" | custom-call | tf_op jit(solution)/shard_map/jit(_solve_triangular)/triangular_solve | solution.py:30
  314.2 11.7 %cholesky.358 = f32[128,128]{1,0:T(8,128)S(1)} custom-call(f32[128,128]{1,0:T(8,128)S(1)} %cholesky.439), custom_call_target="Cholesky" | custom-call | tf_op jit(solution)/shard_map/jit(cholesky)/cholesky | solution.py:34
  327.0 10.0 %custom-call.31 = f32[1,128,128]{1,2,0:T(8,128)S(1)} custom-call(f32[1,128,128]{2,1,0:T(8,128)S(1)} %get-tuple-element.53), custom_call_target="InvertDiagBlocksLowerTriangular" | custom-call | tf_op jit(solution)/shard_map/jit(cholesky)/cholesky | solution.py:34
  340.2 11.7 %cholesky.377 = f32[128,128]{1,0:T(8,128)S(1)} custom-call(f32[128,128]{1,0:T(8,128)S(1)} %cholesky.443), custom_call_target="Cholesky" | custom-call | tf_op jit(solution)/shard_map/jit(cholesky)/cholesky | solution.py:34
  352.5 9.8 %custom-call.32 = f32[1,128,128]{1,2,0:T(8,128)S(1)} custom-call(f32[1,128,128]{2,1,0:T(8,128)S(1)} %get-tuple-element.50), custom_call_target="InvertDiagBlocksLowerTriangular" | custom-call | tf_op jit(solution)/shard_map/jit(cholesky)/cholesky | solution.py:34
  364.7 11.7 %cholesky.398 = f32[128,128]{1,0:T(8,128)S(1)} custom-call(f32[128,128]{1,0:T(8,128)S(1)} %cholesky.448), custom_call_target="Cholesky" | custom-call | tf_op jit(solution)/shard_map/jit(cholesky)/cholesky | solution.py:34
  377.1 10.0 %custom-call.33 = f32[1,128,128]{1,2,0:T(8,128)S(1)} custom-call(f32[1,128,128]{2,1,0:T(8,128)S(1)} %get-tuple-element.47), custom_call_target="InvertDiagBlocksLowerTriangular" | custom-call | tf_op jit(solution)/shard_map/jit(cholesky)/cholesky | solution.py:34
  389.3 11.7 %cholesky.415 = f32[128,128]{1,0:T(8,128)S(1)} custom-call(f32[128,128]{1,0:T(8,128)S(1)} %convolution_subtract_fusion.11), custom_call_target="Cholesky" | custom-call | tf_op jit(solution)/shard_map/jit(cholesky)/cholesky | solution.py:34
  409.4 11.7 %while.5 = (s32[]{:T(128)}, f32[512,512]{1,0:T(8,128)}, s32[4,2]{0,1:T(2,128)S(1)}, f32[4,128,128]{2,1,0:T(8,128)S(1)}, s32[]{:T(128)}) while((s32[]{:T(128)}, f32[512,512]{1,0:T(8,128)}, s32[4,2]{0,1:T(2,128)S(1)}, f32[4,128,128]{2,1,0:T(8,128)S(1)}, s32[]{:T(128)}) %tuple.69), condition=%wide.while_cond.clone, body=%wide.while_body.clone.sunk | while | flops 2 | bytes 131181 | solution.py:30
  421.1 39.7 %custom-call.34 = f32[4,128,128]{1,2,0:T(8,128)S(1)} custom-call(f32[4,128,128]{2,1,0:T(8,128)S(1)} %get-tuple-element.19), custom_call_target="InvertDiagBlocksLowerTriangular" | custom-call | tf_op jit(solution)/shard_map/jit(_solve_triangular)/triangular_solve | solution.py:30
  511.5 31.7 %subtract_select_fusion = f32[2048,1024]{1,0:T(8,128)} fusion(f32[2048,1024]{1,0:T(8,128)} %param.4, pred[1024]{0:T(1024)(128)(4,1)S(1)} %get-tuple-element.69, pred[2048]{0:T(1024)(128)(4,1)S(1)} %get-tuple-element.71, f32[512,1024]{1,0:T(8,128)S(1)} %copy-done.11, f32[512,1024]{1,0:T(8,128)S(1)} %copy-done.3, f32[512,2048]{1,0:T(8,128)S(1)} %fusion.7, ...), kind=kOutput, calls=%fused_computation.8 | convolution fusion | flops 25779240960 | bytes 29363200 | tf_op jit(solution)/shard_map/dot_general | solution.py:17
  (161 shorter events, 170.3 us)
Async XLA Ops:
  7.2 18.1 %slice-start = ((f32[2048,1024]{1,0:T(8,128)}), f32[2048,64]{1,0:T(8,128)S(1)}, s32[]{:S(2)}) async-start(f32[2048,1024]{1,0:T(8,128)} %param.4), calls=%async_computation.2 | async-start | bytes 2097152 | tf_op jit(solution)/shard_map/slice | solution.py:56
  7.2 74.6 %all-gather.6.cloned.1.call-start = ((), (), s32[]{:S(2)}) async-start(), calls=%async_computation.1 | async-start | bytes 4227072 | tf_op jit(solution)/shard_map/all_gather | solution.py:53
  8.9 474.1 %all-gather.4.cloned.1.call-start = ((), (), s32[]{:S(2)}) async-start(), calls=%async_computation | async-start | bytes 8912896 | tf_op jit(solution)/shard_map/all_gather | solution.py:56
  13.4 9.2 %collective-permute-start = (f32[128,1024]{1,0:T(8,128)S(1)}, f32[128,1024]{1,0:T(8,128)S(1)}, u32[]{:S(2)}, u32[]{:S(2)}) collective-permute-start(f32[128,1024]{1,0:T(8,128)S(1)} %get-tuple-element.40), channel_id=1, source_target_pairs={{0,16},{16,32},{32,48},{48,64},{64,80},{80,96},{96,112},{112,0},{1... | collective-permute-start | bytes 1572872 | tf_op jit(solution)/shard_map/ppermute | solution.py:72
  16.4 8.6 %collective-permute-start.1 = (f32[128,1024]{1,0:T(8,128)S(1)}, f32[128,1024]{1,0:T(8,128)S(1)}, u32[]{:S(2)}, u32[]{:S(2)}) collective-permute-start(f32[128,1024]{1,0:T(8,128)S(1)} %get-tuple-element.40), channel_id=1, source_target_pairs={{0,112},{16,0},{32,16},{48,32},{64,48},{80,64},{96,80},{112,96},{1... | collective-permute-start | bytes 1572872 | tf_op jit(solution)/shard_map/ppermute | solution.py:77
  22.5 11.4 %copy-start.12 = (f32[128,1024]{1,0:T(8,128)}, f32[128,1024]{1,0:T(8,128)S(1)}, u32[]{:S(2)}) copy-start(f32[128,1024]{1,0:T(8,128)S(1)} %collective-permute-done) | copy-start | bytes 1572868
  22.5 8.8 %collective-permute-start.2 = (f32[128,1024]{1,0:T(8,128)S(1)}, f32[128,1024]{1,0:T(8,128)}, u32[]{:S(2)}, u32[]{:S(2)}) collective-permute-start(f32[128,1024]{1,0:T(8,128)S(1)} %collective-permute-done), channel_id=1, source_target_pairs={{0,16},{16,32},{32,48},{48,64},{64,80},{80,96},{96,112},{112,0},{1... | collective-permute-start | bytes 1572872 | tf_op jit(solution)/shard_map/ppermute | solution.py:72
  25.0 9.2 %collective-permute-start.3 = (f32[128,1024]{1,0:T(8,128)S(1)}, f32[128,1024]{1,0:T(8,128)S(1)}, u32[]{:S(2)}, u32[]{:S(2)}) collective-permute-start(f32[128,1024]{1,0:T(8,128)S(1)} %collective-permute-done.1), channel_id=1, source_target_pairs={{0,112},{16,0},{32,16},{48,32},{64,48},{80,64},{96,80},{112,96},{1... | collective-permute-start | bytes 1572872 | tf_op jit(solution)/shard_map/ppermute | solution.py:77
  31.3 9.1 %collective-permute-start.4 = (f32[128,1024]{1,0:T(8,128)}, f32[128,1024]{1,0:T(8,128)S(1)}, u32[]{:S(2)}, u32[]{:S(2)}) collective-permute-start(f32[128,1024]{1,0:T(8,128)} %collective-permute-done.2), channel_id=1, source_target_pairs={{0,16},{16,32},{32,48},{48,64},{64,80},{80,96},{96,112},{112,0},{1... | collective-permute-start | bytes 1572872 | tf_op jit(solution)/shard_map/ppermute | solution.py:72
  34.2 13.0 %collective-permute-start.5 = (f32[128,1024]{1,0:T(8,128)S(1)}, f32[128,1024]{1,0:T(8,128)S(1)}, u32[]{:S(2)}, u32[]{:S(2)}) collective-permute-start(f32[128,1024]{1,0:T(8,128)S(1)} %collective-permute-done.3), channel_id=1, source_target_pairs={{0,112},{16,0},{32,16},{48,32},{64,48},{80,64},{96,80},{112,96},{1... | collective-permute-start | bytes 1572872 | tf_op jit(solution)/shard_map/ppermute | solution.py:77
  40.4 9.2 %collective-permute-start.6 = (f32[128,1024]{1,0:T(8,128)S(1)}, f32[128,1024]{1,0:T(8,128)S(1)}, u32[]{:S(2)}, u32[]{:S(2)}) collective-permute-start(f32[128,1024]{1,0:T(8,128)S(1)} %collective-permute-done.4), channel_id=1, source_target_pairs={{0,16},{16,32},{32,48},{48,64},{64,80},{80,96},{96,112},{112,0},{1... | collective-permute-start | bytes 1572872 | tf_op jit(solution)/shard_map/ppermute | solution.py:72
  157.2 1.0 copy-start.10
  298.0 6.1 %copy-start = (f32[1024,1024]{0,1:T(8,128)S(1)}, f32[1024,1024]{0,1:T(8,128)}, u32[]{:S(2)}) copy-start(f32[1024,1024]{0,1:T(8,128)} %reshape.140) | copy-start | bytes 12582916
  304.1 7.3 %copy-start.7 = (f32[128,512]{1,0:T(8,128)}, f32[128,512]{1,0:T(8,128)S(1)}, u32[]{:S(2)}) copy-start(f32[128,512]{1,0:T(8,128)S(1)} %fusion.59) | copy-start | bytes 786436
  313.2 1.0 copy-start.9
  460.9 0.7 copy-start.13
  460.9 8.9 %copy-start.4 = (f32[2,8,32,1024]{3,2,1,0:T(8,128)S(1)}, f32[2,8,32,1024]{3,2,1,0:T(8,128)}, u32[]{:S(2)}) copy-start(f32[2,8,32,1024]{3,2,1,0:T(8,128)} %copy.26) | copy-start | bytes 6291460
  465.4 8.9 %copy-start.1 = (f32[2,8,32,1024]{3,2,1,0:T(8,128)S(1)}, f32[2,8,32,1024]{3,2,1,0:T(8,128)}, u32[]{:S(2)}) copy-start(f32[2,8,32,1024]{3,2,1,0:T(8,128)} %copy.27) | copy-start | bytes 6291460
  466.9 11.1 %copy-start.5 = (f32[128,512]{1,0:T(8,128)}, f32[128,512]{1,0:T(8,128)S(1)}, u32[]{:S(2)}) copy-start(f32[128,512]{1,0:T(8,128)S(1)} %fusion.54) | copy-start | bytes 786436
  474.3 3.5 copy-start.2
  483.0 4.0 copy-start.8
  494.2 7.8 %copy-start.6 = (f32[128,512]{1,0:T(8,128)S(1)}, f32[128,512]{1,0:T(8,128)}, u32[]{:S(2)}) copy-start(f32[128,512]{1,0:T(8,128)} %copy-done.5) | copy-start | bytes 786436
  509.1 1.8 copy-start.3
  509.1 2.4 copy-start.11
Sparse Core Ops, SparseCore 0:
  11.1 70.5 all-gather.5
  83.9 67.6 all-gather.3
